TPU v7x, 32 devices: a whole 2x2x4 slice. The times are simulated.
32 devices in a mesh: group: 2 (over x), tm: 16 (over z, y, core).
Axes of the slice: x: 2, y: 2, z: 4, core: 2. Of those that a mesh axis runs over, the one named last changes fastest.
Arguments:
- records: float32 [256, 262144], P('group', 'tm'), parts along dimension 0, may hold values from -6 to 6
- labels: int32 [256], P('group'), parts along dimension 0, may hold values from 0 to 1
- first_weight: bfloat16 [131072, 1024], P('tm'), may hold values from -0.015625 to 0.015625
- first_bias: float32 [1024], replicated, may hold values from -3 to 3
- second_weight: float32 [1024], replicated, may hold values from -0.1875 to 0.1875
- second_bias: float32 [1], replicated, may hold values from -3 to 3
Outputs:
- loss: float32 [2], P('group'), parts along dimension 0
- grad_first: float32 [262144, 1024], P(('group', 'tm')), parts along dimension 0
- grad_bias: float32 [2048], P('group'), parts along dimension 0
- grad_second: float32 [2048], P('group'), parts along dimension 0
- grad_out_bias: float32 [2], P('group'), parts along dimension 0
There are 2 independent parts, one for each index of `group`. A program takes and returns all parts, laid end to end along the dimension named above; an argument that names none is the same for every part. Nothing has to cross between parts.
All inputs are finite; a program needn't handle non-finite values.
Results may differ from a plain program's by a relative error of at most 0.0079.
Values may be sent and summed in bfloat16 or wider, within the bound.
No kernel may reach another device: no remote copies, remote signals or barrier semaphores. Data moves between devices by JAX's collectives and lax.ppermute only.
A program may use at most 192 MiB of HBM per device.

v0:
```python
import math
import jax
import jax.numpy as jnp
from jax import lax
from jax.sharding import PartitionSpec as P

N1 = 512
N2 = 512


def first_table(count):
    rows = jnp.arange(count, dtype=jnp.int32)[:, None]
    cols = jnp.arange(count, dtype=jnp.int32)[None, :]
    angle = 2.0 * math.pi / count * (rows * cols % count).astype(jnp.float32)
    scale = 1.0 / math.sqrt(count)
    return jnp.concatenate([jnp.cos(angle) * scale, -jnp.sin(angle) * scale], 0).astype(
        jnp.bfloat16
    )


def second_table(count):
    rows = jnp.arange(count, dtype=jnp.int32)[:, None]
    cols = jnp.arange(count // 2, dtype=jnp.int32)[None, :]
    angle = 2.0 * math.pi / count * (rows * cols % count).astype(jnp.float32)
    scale = 1.0 / math.sqrt(count)
    cosine = jnp.cos(angle) * scale
    sine = jnp.sin(angle) * scale
    upper = jnp.concatenate([cosine, -sine], 1)
    lower = jnp.concatenate([sine, cosine], 1)
    return jnp.concatenate([upper, lower], 0).astype(jnp.bfloat16)


def on_device(records, labels, first_weight, first_bias, second_weight, second_bias):
    devices = lax.axis_size("tm")
    slow_rows = N2 // devices
    fast_cols = N1 // devices
    table_one = first_table(N2)
    table_two = second_table(N1)
    total_len = N1 * N2
    count_rec = records.shape[0]
    samples = records.astype(jnp.bfloat16).reshape(count_rec, slow_rows, N1)
    samples = jnp.transpose(samples, (0, 2, 1))
    partial_value = jnp.einsum(
        "rcn,kn->rck",
        lax.all_to_all(samples, "tm", split_axis=1, concat_axis=2, tiled=True),
        table_one,
        preferred_element_type=jnp.float32,
    )
    real_part = partial_value[:, :, :N2]
    imag_part = partial_value[:, :, N2:]
    fast = lax.axis_index("tm") * fast_cols + jnp.arange(fast_cols, dtype=jnp.int32)
    slow = jnp.arange(N2, dtype=jnp.int32)
    phase = (
        2.0 * math.pi / total_len * (fast[:, None] * slow[None, :] % total_len).astype(jnp.float32)
    )
    cosine = jnp.cos(phase)[None]
    sine = jnp.sin(phase)[None]
    twisted_re = real_part * cosine + imag_part * sine
    twisted_im = imag_part * cosine - real_part * sine
    stacked = jnp.stack([twisted_re, twisted_im], 1).astype(jnp.bfloat16)
    twisted = jnp.transpose(stacked, (0, 3, 1, 2))
    block = lax.all_to_all(twisted, "tm", split_axis=1, concat_axis=3, tiled=True)
    count = block.shape[0]
    joined = block.reshape(count, block.shape[1], 2 * N1)
    bins = jnp.einsum("rbm,mf->rbf", joined, table_two, preferred_element_type=jnp.float32)
    power = bins[:, :, : N1 // 2] ** 2 + bins[:, :, N1 // 2 :] ** 2
    features = jnp.log(1.0 + power).astype(jnp.bfloat16).reshape(count, block.shape[1] * (N1 // 2))
    target = labels.astype(jnp.float32)
    partial_sums = jnp.dot(features, first_weight, preferred_element_type=jnp.float32)
    pre = lax.psum(partial_sums, "tm") + first_bias[None, :]
    gate = jax.nn.sigmoid(pre)
    hidden = pre * gate
    logit = jnp.sum(hidden * second_weight[None, :], 1) + second_bias[0]
    dlogit = jax.nn.sigmoid(logit) - target
    dpre = (dlogit[:, None] * second_weight[None, :] * gate * (1.0 + pre * (1.0 - gate))).astype(
        jnp.bfloat16
    )
    grad_first = lax.dot_general(
        features, dpre, (((0,), (0,)), ((), ())), preferred_element_type=jnp.float32
    )
    grad_bias = jnp.sum(dpre.astype(jnp.float32), 0)
    grad_second = jnp.sum(hidden * dlogit[:, None], 0)
    loss = jnp.mean(jnp.log(1.0 + jnp.exp(logit)) - target * logit).reshape(1)
    grad_out_bias = jnp.sum(dlogit).reshape(1)
    return (loss, grad_first, grad_bias, grad_second, grad_out_bias)


def solution(mesh):
    return jax.shard_map(
        on_device,
        mesh=mesh,
        in_specs=(P("group", "tm"), P("group"), P("tm", None), P(), P(), P()),
        out_specs=(P("group"), P(("group", "tm"), None), P("group"), P("group"), P("group")),
        check_vma=False,
    )
```

profile of v0, /device:TPU:1, one launch (start us, length us, event | category | flops | bytes accessed | tf_op | source)
XLA Modules:
  0.0 488.0 jit_solution(15323579355672855773)
XLA Ops:
  7.2 7.2 %copy.31 = bf16[128,16384]{0,1:T(8,128)(2,1)} copy(f32[128,16384]{1,0:T(8,128)} %param.6) | data formatting | bytes 12582912 | tf_op args[0]
  14.4 6.9 %copy.32 = bf16[128,512,32]{0,2,1:T(8,128)(2,1)} copy(bf16[128,512,32]{0,1,2:T(8,128)(2,1)} %bitcast.39) | data formatting | bytes 8388608 | tf_op jit(solution)/shard_map/transpose | solution.py:42
  21.2 7.3 %all-to-all-start = ((bf16[128,512,32]{0,2,1:T(8,128)(2,1)}), bf16[128,512,32]{0,2,1:T(8,128)(2,1)}, u32[]{:S(2)}, u32[]{:S(2)}) async-start(bf16[128,512,32]{0,2,1:T(8,128)(2,1)} %copy.32), calls=%async_computation | async-start | bytes 8388608 | tf_op jit(solution)/shard_map/all_to_all | solution.py:45
  28.6 4.4 multiply_convert_fusion
  33.0 0.3 fusion.36
  33.3 73.3 %all-to-all-done = bf16[128,512,32]{0,2,1:T(8,128)(2,1)} async-done(((bf16[128,512,32]{0,2,1:T(8,128)(2,1)}), bf16[128,512,32]{0,2,1:T(8,128)(2,1)}, u32[]{:S(2)}, u32[]{:S(2)}) %all-to-all-start) | async-done | bytes 4194336 | tf_op jit(solution)/shard_map/all_to_all | solution.py:45
  106.7 3.4 copy.33
  110.1 4.5 convolution_bitcast_fusion
  114.7 5.8 %fusion = (bf16[128,1,32,512]{0,3,2,1:T(8,128)(2,1)S(1)}, bf16[128,1,32,512]{0,3,2,1:T(8,128)(2,1)}) fusion(f32[128,32,1024]{0,2,1:T(8,128)S(1)} %convolution_bitcast_fusion, f32[32,512]{1,0:T(8,128)S(1)} %get-tuple-element.14, f32[32,512]{1,0:T(8,128)S(1)} %get-tuple-element.13), kind=kLoop, calls=%fused_computation.4 | loop fusion | flops 16777216 | bytes 25296896 | tf_op jit(solution)/shard_map/stack | solution.py:60
  120.5 6.3 %maximum_bitcast_fusion = bf16[128,512,2,32]{0,1,3,2:T(8,128)(2,1)} fusion(bf16[128,1,32,512]{0,3,2,1:T(8,128)(2,1)} %get-tuple-element.10, bf16[128,1,32,512]{0,3,2,1:T(8,128)(2,1)S(1)} %get-tuple-element.9), kind=kLoop, calls=%fused_computation.1 | loop fusion | flops 4194304 | bytes 16777216 | tf_op jit(solution)/shard_map/transpose | solution.py:61
  126.8 12.0 %copy.35 = bf16[128,512,2,32]{0,3,2,1:T(8,128)(2,1)} copy(bf16[128,512,2,32]{0,1,3,2:T(8,128)(2,1)} %maximum_bitcast_fusion) | data formatting | bytes 16777216 | tf_op jit(solution)/shard_map/transpose | solution.py:61
  138.8 19.3 %all-to-all-start.1 = ((bf16[128,512,2,32]{0,3,2,1:T(8,128)(2,1)}), bf16[128,512,2,32]{0,3,2,1:T(8,128)(2,1)}, u32[]{:S(2)}, u32[]{:S(2)}) async-start(bf16[128,512,2,32]{0,3,2,1:T(8,128)(2,1)} %copy.35), calls=%async_computation.1 | async-start | bytes 16777216 | tf_op jit(solution)/shard_map/all_to_all | solution.py:62
  158.1 0.0 all-reduce.2.cloned.1.call-start
  158.2 2.2 fusion.28
  160.4 2.2 negate_convert_fusion
  162.6 146.6 %all-to-all-done.1 = bf16[128,512,2,32]{0,3,2,1:T(8,128)(2,1)} async-done(((bf16[128,512,2,32]{0,3,2,1:T(8,128)(2,1)}), bf16[128,512,2,32]{0,3,2,1:T(8,128)(2,1)}, u32[]{:S(2)}, u32[]{:S(2)}) %all-to-all-start.1) | async-done | bytes 8388640 | tf_op jit(solution)/shard_map/all_to_all | solution.py:62
  309.2 9.0 %copy.36 = bf16[128,32,2,16,32]{0,4,3,2,1:T(8,128)(2,1)} copy(bf16[128,32,2,16,32]{0,4,2,1,3:T(8,128)(2,1)} %bitcast.11) | data formatting | bytes 16777216 | tf_op jit(solution)/shard_map/all_to_all | solution.py:62
  318.2 7.0 %fusion.11 = f32[128,32,512]{2,0,1:T(8,128)S(1)} fusion(bf16[128,32,1024]{0,2,1:T(8,128)(2,1)} %bitcast.36, bf16[512,256]{1,0:T(8,128)(2,1)S(1)} %get-tuple-element.18, bf16[512,256]{1,0:T(8,128)(2,1)S(1)} %fusion.28, bf16[512,256]{1,0:T(8,128)(2,1)S(1)} %get-tuple-element.17), kind=kOutput, calls=%fused_computation.22 | convolution fusion | flops 4299161600 | bytes 17563648 | tf_op jit(solution)/shard_map/rbm,mf->rbf/dot_general | solution.py:65
  325.2 2.3 fusion.5
  327.5 3.2 copy.38
  330.7 0.0 copy-start
  330.7 0.0 copy-start.1
  330.7 0.0 copy-start.2
  330.7 8.9 %fusion.40 = f32[128,1024]{1,0:T(8,128)} fusion(bf16[128,8192]{0,1:T(8,128)(2,1)S(1)} %bitcast.37, bf16[8192,1024]{1,0:T(8,128)(2,1)} %param.8), kind=kOutput, calls=%fused_computation.70 | convolution fusion | flops 2147483648 | bytes 19398656 | tf_op jit(solution)/shard_map/dot_general | solution.py:69
  339.7 0.0 all-reduce.2.cloned.1.call-update
  340.3 121.1 %all-reduce.2.cloned.1.call-done = f32[128,1024]{1,0:T(8,128)} async-done(((f32[128,1024]{1,0:T(8,128)}), f32[128,1024]{1,0:T(8,128)}) %all-reduce.2.cloned.1.call-update) | async-done | bytes 524304 | tf_op jit(solution)/shard_map/psum | solution.py:70
  461.4 0.0 copy-done
  461.4 0.0 copy-done.1
  461.4 1.3 multiply_reduce_fusion.1
  462.7 0.0 copy-done.2
  462.7 0.7 fusion.39
  463.4 1.9 convert_reduce_fusion
  465.4 14.0 %fusion.41 = f32[8192,1024]{1,0:T(8,128)} fusion(bf16[128,8192]{0,1:T(8,128)(2,1)S(1)} %bitcast.38, bf16[128,1024]{1,0:T(8,128)(2,1)S(1)} %get-tuple-element.8), kind=kOutput, calls=%fused_computation.71 | convolution fusion | flops 2147483648 | bytes 35913728 | tf_op jit(solution)/shard_map/dot_general | solution.py:78
  (1 shorter events, 0.0 us)
Async XLA Ops:
  21.2 85.4 %all-to-all-start = ((bf16[128,512,32]{0,2,1:T(8,128)(2,1)}), bf16[128,512,32]{0,2,1:T(8,128)(2,1)}, u32[]{:S(2)}, u32[]{:S(2)}) async-start(bf16[128,512,32]{0,2,1:T(8,128)(2,1)} %copy.32), calls=%async_computation | async-start | bytes 8388608 | tf_op jit(solution)/shard_map/all_to_all | solution.py:45
  138.8 170.4 %all-to-all-start.1 = ((bf16[128,512,2,32]{0,3,2,1:T(8,128)(2,1)}), bf16[128,512,2,32]{0,3,2,1:T(8,128)(2,1)}, u32[]{:S(2)}, u32[]{:S(2)}) async-start(bf16[128,512,2,32]{0,3,2,1:T(8,128)(2,1)} %copy.35), calls=%async_computation.1 | async-start | bytes 16777216 | tf_op jit(solution)/shard_map/all_to_all | solution.py:62
  158.1 303.3 %all-reduce.2.cloned.1.call-start = ((), (), s32[]{:S(2)}) async-start(), calls=%async_computation.2 | async-start | bytes 1048576 | tf_op jit(solution)/shard_map/psum | solution.py:70
  330.7 130.7 %copy-start = (f32[1024]{0:T(1024)S(1)}, f32[1024]{0:T(1024)}, u32[]{:S(2)}) copy-start(f32[1024]{0:T(1024)} %param.10) | copy-start | bytes 12292
  330.7 130.7 %copy-start.1 = (f32[1024]{0:T(1024)S(1)}, f32[1024]{0:T(1024)}, u32[]{:S(2)}) copy-start(f32[1024]{0:T(1024)} %param.9) | copy-start | bytes 12292
  330.7 132.0 %copy-start.2 = (s32[128]{0:T(128)S(1)}, s32[128]{0:T(128)}, u32[]{:S(2)}) copy-start(s32[128]{0:T(128)} %param.7) | copy-start | bytes 1540
Sparse Core Ops, SparseCore 0:
  339.8 121.5 all-reduce.1
where the time goes:
time: 489 us; the launch traced here: 488 us
  waiting for transfers between devices  341 us (70%)
  local copies, waits for them, and re-layouts  41.7 us (9%)
  matrix products  34.5 us (7%)
  other arithmetic  27.5 us (6%)
  starting transfers between devices  26.7 us (5%)
  between operations  16.6 us (3%)
    all_to_all x1, waiting for transfers between devices, on_device(): lax.all_to_all(twisted, 'tm', split_axis=1, concat_axis=3, tiled=True)  147 us
    psum x1, waiting for transfers between devices, on_device(): pre = lax.psum(partial_sums, 'tm') + first_bias[None, :]  121 us
    all_to_all x1, waiting for transfers between devices, on_device(): lax.all_to_all(samples, 'tm', split_axis=1, concat_axis=2, tiled=True)  73.3 us
    all_to_all x1, starting transfers between devices, on_device(): lax.all_to_all(twisted, 'tm', split_axis=1, concat_axis=3, tiled=True)  19.3 us
    dot_general x1, matrix products, on_device(): lax.dot_general(features, dpre, (((0,), (0,)), ((), ())), preferred_eleme...  14 us
    transpose x1, local copies, waits for them, and re-layouts, on_device(): twisted = jnp.transpose(stacked, (0, 3, 1, 2))  12 us
  transfers between devices with their start and end apart: 3, of which 3 were waited for; matrix products, arithmetic and copies ran while one was open for 2% of the time, Pallas kernels for 0%

commit v1 on v0

--- a/solution.py
+++ b/solution.py
@@ -59,7 +59,10 @@
     twisted_im = imag_part * cosine - real_part * sine
     stacked = jnp.stack([twisted_re, twisted_im], 1).astype(jnp.bfloat16)
     twisted = jnp.transpose(stacked, (0, 3, 1, 2))
-    block = lax.all_to_all(twisted, "tm", split_axis=1, concat_axis=3, tiled=True)
+    block = jnp.concatenate(
+        lax.all_to_all(jnp.stack(jnp.split(twisted, lax.axis_size("tm"), axis=1)), "tm", 0, 0),
+        axis=3,
+    )
     count = block.shape[0]
     joined = block.reshape(count, block.shape[1], 2 * N1)
     bins = jnp.einsum("rbm,mf->rbf", joined, table_two, preferred_element_type=jnp.float32)

time: 489 us -> 509 us (1.041)
  local copies, waits for them, and re-layouts: 41.7 us -> 61.1 us
    unnamed x7 -> x22, local copies, waits for them, and re-layouts: 7.25 us -> 35.7 us
    transpose x1 -> x0, local copies, waits for them, and re-layouts: 12 us -> none  [on_device(): twisted = jnp.transpose(stacked, (0, 3, 1, 2))]
    reshape x0 -> x1, local copies, waits for them, and re-layouts: none -> 10 us  [on_device(): jnp.concatenate(lax.all_to_all(jnp.stack(jnp.split(twisted, lax.axis_size...]
    all_to_all x1 -> x0, local copies, waits for them, and re-layouts: 8.97 us -> none  [on_device(): lax.all_to_all(twisted, 'tm', split_axis=1, concat_axis=3, tiled=True)]
where the time goes in v1:
time: 509 us; the launch traced here: 507 us
  waiting for transfers between devices  341 us (67%)
  local copies, waits for them, and re-layouts  61.1 us (12%)
  matrix products  34.5 us (7%)
  other arithmetic  27.3 us (5%)
  starting transfers between devices  26.9 us (5%)
  between operations  16.6 us (3%)
    all_to_all x1, waiting for transfers between devices, on_device(): lax.all_to_all(jnp.stack(jnp.split(twisted, lax.axis_size('tm'), axis=1))...  147 us
    psum x1, waiting for transfers between devices, on_device(): pre = lax.psum(partial_sums, 'tm') + first_bias[None, :]  121 us
    all_to_all x1, waiting for transfers between devices, on_device(): lax.all_to_all(samples, 'tm', split_axis=1, concat_axis=2, tiled=True)  73.3 us
    unnamed x22, local copies, waits for them, and re-layouts  35.7 us
    all_to_all x1, starting transfers between devices, on_device(): lax.all_to_all(jnp.stack(jnp.split(twisted, lax.axis_size('tm'), axis=1))...  19.3 us
    dot_general x1, matrix products, on_device(): lax.dot_general(features, dpre, (((0,), (0,)), ((), ())), preferred_eleme...  14 us
  transfers between devices with their start and end apart: 3, of which 3 were waited for; matrix products, arithmetic and copies ran while one was open for 2% of the time, Pallas kernels for 0%

profile of v1, /device:TPU:1, one launch (start us, length us, event | category | flops | bytes accessed | tf_op | source)
XLA Modules:
  0.0 507.4 jit_solution(13351568037099463998)
XLA Ops:
  7.2 7.2 %copy.23 = bf16[128,16384]{0,1:T(8,128)(2,1)} copy(f32[128,16384]{1,0:T(8,128)} %param.6) | data formatting | bytes 12582912 | tf_op args[0]
  14.4 6.9 %copy.24 = bf16[128,512,32]{0,2,1:T(8,128)(2,1)} copy(bf16[128,512,32]{0,1,2:T(8,128)(2,1)} %bitcast.101) | data formatting | bytes 8388608 | tf_op jit(solution)/shard_map/transpose | solution.py:42
  21.2 7.3 %all-to-all-start = ((bf16[128,512,32]{0,2,1:T(8,128)(2,1)}), bf16[128,512,32]{0,2,1:T(8,128)(2,1)}, u32[]{:S(2)}, u32[]{:S(2)}) async-start(bf16[128,512,32]{0,2,1:T(8,128)(2,1)} %copy.24), calls=%async_computation | async-start | bytes 8388608 | tf_op jit(solution)/shard_map/all_to_all | solution.py:45
  28.6 4.4 multiply_convert_fusion
  33.0 0.3 fusion.52
  33.3 73.3 %all-to-all-done = bf16[128,512,32]{0,2,1:T(8,128)(2,1)} async-done(((bf16[128,512,32]{0,2,1:T(8,128)(2,1)}), bf16[128,512,32]{0,2,1:T(8,128)(2,1)}, u32[]{:S(2)}, u32[]{:S(2)}) %all-to-all-start) | async-done | bytes 4194336 | tf_op jit(solution)/shard_map/all_to_all | solution.py:45
  106.7 3.4 copy.25
  110.1 4.5 convolution_bitcast_fusion
  114.7 5.8 %fusion = (bf16[128,1,32,512]{0,3,2,1:T(8,128)(2,1)S(1)}, bf16[128,1,32,512]{0,3,2,1:T(8,128)(2,1)}) fusion(f32[128,32,1024]{0,2,1:T(8,128)S(1)} %convolution_bitcast_fusion, f32[32,512]{1,0:T(8,128)S(1)} %get-tuple-element.14, f32[32,512]{1,0:T(8,128)S(1)} %get-tuple-element.13), kind=kLoop, calls=%fused_computation.4 | loop fusion | flops 16777216 | bytes 25296896 | tf_op jit(solution)/shard_map/stack | solution.py:60
  120.5 6.3 %maximum_bitcast_fusion = bf16[128,512,2,32]{0,1,3,2:T(8,128)(2,1)} fusion(bf16[128,1,32,512]{0,3,2,1:T(8,128)(2,1)} %get-tuple-element.10, bf16[128,1,32,512]{0,3,2,1:T(8,128)(2,1)S(1)} %get-tuple-element.9), kind=kLoop, calls=%fused_computation.1 | loop fusion | flops 4194304 | bytes 16777216 | tf_op jit(solution)/shard_map/transpose | solution.py:61
  126.8 1.9 fusion.39
  128.8 2.0 fusion.38
  130.7 1.9 fusion.37
  132.6 1.9 fusion.36
  134.5 1.9 fusion.35
  136.4 1.9 fusion.34
  138.3 1.9 fusion.33
  140.2 1.9 fusion.32
  142.0 1.9 fusion.31
  144.0 1.9 fusion.30
  145.9 1.9 fusion.29
  147.7 1.9 fusion.28
  149.6 1.9 fusion.27
  151.5 1.9 fusion.26
  153.4 1.9 fusion.25
  155.3 1.9 fusion.24
  157.2 19.3 %all-to-all-start.1 = ((bf16[16,128,32,2,32]{1,2,4,3,0:T(8,128)(2,1)}), bf16[16,128,32,2,32]{1,2,4,3,0:T(8,128)(2,1)}, u32[]{:S(2)}, u32[]{:S(2)}) async-start(bf16[16,128,32,2,32]{1,2,4,3,0:T(8,128)(2,1)} %fusion.24), calls=%async_computation.1 | async-start | bytes 16777216 | tf_op jit(solution)/shard_map/all_to_all | solution.py:63
  176.5 0.2 all-reduce.2.cloned.1.call-start
  176.7 2.0 fusion.44
  178.7 2.2 negate_convert_fusion
  180.9 146.7 %all-to-all-done.1 = bf16[16,128,32,2,32]{1,2,4,3,0:T(8,128)(2,1)} async-done(((bf16[16,128,32,2,32]{1,2,4,3,0:T(8,128)(2,1)}), bf16[16,128,32,2,32]{1,2,4,3,0:T(8,128)(2,1)}, u32[]{:S(2)}, u32[]{:S(2)}) %all-to-all-start.1) | async-done | bytes 8388640 | tf_op jit(solution)/shard_map/all_to_all | solution.py:63
  327.6 10.0 %copy.27 = bf16[128,32,2,16,32]{0,4,3,2,1:T(8,128)(2,1)} copy(bf16[128,32,2,16,32]{0,1,4,2,3:T(8,128)(2,1)} %bitcast.26) | data formatting | bytes 16777216 | tf_op jit(solution)/shard_map/reshape | solution.py:62
  337.6 7.0 %fusion.11 = f32[128,32,512]{2,0,1:T(8,128)S(1)} fusion(bf16[128,32,1024]{0,2,1:T(8,128)(2,1)} %bitcast.98, bf16[512,256]{1,0:T(8,128)(2,1)S(1)} %get-tuple-element.18, bf16[512,256]{1,0:T(8,128)(2,1)S(1)} %fusion.44, bf16[512,256]{1,0:T(8,128)(2,1)S(1)} %get-tuple-element.17), kind=kOutput, calls=%fused_computation.22 | convolution fusion | flops 4299161600 | bytes 17563648 | tf_op jit(solution)/shard_map/rbm,mf->rbf/dot_general | solution.py:68
  344.6 2.3 fusion.5
  346.9 3.2 copy.29
  350.1 0.0 copy-start
  350.1 0.0 copy-start.1
  350.1 0.0 copy-start.2
  350.1 8.9 %fusion.56 = f32[128,1024]{1,0:T(8,128)} fusion(bf16[128,8192]{0,1:T(8,128)(2,1)S(1)} %bitcast.99, bf16[8192,1024]{1,0:T(8,128)(2,1)} %param.8), kind=kOutput, calls=%fused_computation.102 | convolution fusion | flops 2147483648 | bytes 19398656 | tf_op jit(solution)/shard_map/dot_general | solution.py:72
  359.1 0.0 all-reduce.2.cloned.1.call-update
  359.7 121.1 %all-reduce.2.cloned.1.call-done = f32[128,1024]{1,0:T(8,128)} async-done(((f32[128,1024]{1,0:T(8,128)}), f32[128,1024]{1,0:T(8,128)}) %all-reduce.2.cloned.1.call-update) | async-done | bytes 524304 | tf_op jit(solution)/shard_map/psum | solution.py:73
  480.8 0.0 copy-done
  480.8 0.0 copy-done.1
  480.8 1.3 multiply_reduce_fusion.1
  482.1 0.0 copy-done.2
  482.1 0.7 fusion.55
  482.8 1.9 convert_reduce_fusion
  484.7 14.0 %fusion.57 = f32[8192,1024]{1,0:T(8,128)} fusion(bf16[128,8192]{0,1:T(8,128)(2,1)S(1)} %bitcast.100, bf16[128,1024]{1,0:T(8,128)(2,1)S(1)} %get-tuple-element.8), kind=kOutput, calls=%fused_computation.103 | convolution fusion | flops 2147483648 | bytes 35913728 | tf_op jit(solution)/shard_map/dot_general | solution.py:81
  (1 shorter events, 0.0 us)
Async XLA Ops:
  21.2 85.4 %all-to-all-start = ((bf16[128,512,32]{0,2,1:T(8,128)(2,1)}), bf16[128,512,32]{0,2,1:T(8,128)(2,1)}, u32[]{:S(2)}, u32[]{:S(2)}) async-start(bf16[128,512,32]{0,2,1:T(8,128)(2,1)} %copy.24), calls=%async_computation | async-start | bytes 8388608 | tf_op jit(solution)/shard_map/all_to_all | solution.py:45
  157.2 170.4 %all-to-all-start.1 = ((bf16[16,128,32,2,32]{1,2,4,3,0:T(8,128)(2,1)}), bf16[16,128,32,2,32]{1,2,4,3,0:T(8,128)(2,1)}, u32[]{:S(2)}, u32[]{:S(2)}) async-start(bf16[16,128,32,2,32]{1,2,4,3,0:T(8,128)(2,1)} %fusion.24), calls=%async_computation.1 | async-start | bytes 16777216 | tf_op jit(solution)/shard_map/all_to_all | solution.py:63
  176.5 304.4 %all-reduce.2.cloned.1.call-start = ((), (), s32[]{:S(2)}) async-start(), calls=%async_computation.2 | async-start | bytes 1048576 | tf_op jit(solution)/shard_map/psum | solution.py:73
  350.1 130.7 %copy-start = (f32[1024]{0:T(1024)S(1)}, f32[1024]{0:T(1024)}, u32[]{:S(2)}) copy-start(f32[1024]{0:T(1024)} %param.10) | copy-start | bytes 12292
  350.1 130.7 %copy-start.1 = (f32[1024]{0:T(1024)S(1)}, f32[1024]{0:T(1024)}, u32[]{:S(2)}) copy-start(f32[1024]{0:T(1024)} %param.9) | copy-start | bytes 12292
  350.1 132.0 %copy-start.2 = (s32[128]{0:T(128)S(1)}, s32[128]{0:T(128)}, u32[]{:S(2)}) copy-start(s32[128]{0:T(128)} %param.7) | copy-start | bytes 1540
Sparse Core Ops, SparseCore 0:
  359.2 121.5 all-reduce.1
